TPU v7x, 32 devices: a whole 2x2x4 slice. The times are simulated.
32 devices in a mesh: replica: 8 (over z, core), shard: 4 (over y, x).
Axes of the slice: x: 2, y: 2, z: 4, core: 2. Of those that a mesh axis runs over, the one named last changes fastest.
Arguments:
- hidden_in: bfloat16 [4, 2048, 2048], P('shard', 'replica'), may hold values from -6 to 6
- piece_index: int32 [4, 2048], P('shard', 'replica'), may hold values from -1 to 7, as said below
- pad_flags: int32 [4, 2048], P('shard', 'replica'), may hold values from 0 to 1, as said below
- cotangent: bfloat16 [4, 2048, 2048], P('shard', 'replica'), may hold values from -6 to 6
- query_weight: bfloat16 [2048, 2048], P('shard'), may hold values from -0.125 to 0.125
- key_weight: bfloat16 [2048, 2048], P('shard'), may hold values from -0.125 to 0.125
- value_weight: bfloat16 [2048, 2048], P('shard'), may hold values from -0.125 to 0.125
- output_weight: bfloat16 [2048, 2048], P('shard'), may hold values from -0.125 to 0.125
- gate_weight: bfloat16 [2048, 8192], P('shard'), may hold values from -0.125 to 0.125
- up_weight: bfloat16 [2048, 8192], P('shard'), may hold values from -0.125 to 0.125
- down_weight: bfloat16 [8192, 2048], P('shard'), may hold values from -0.0625 to 0.0625
- query_gain: bfloat16 [2048], P('shard'), may hold values from 0.25 to 1.75
- key_gain: bfloat16 [2048], P('shard'), may hold values from 0.25 to 1.75
- attention_gain: bfloat16 [2048], P('shard'), may hold values from 0.25 to 1.75
- feed_gain: bfloat16 [2048], P('shard'), may hold values from 0.25 to 1.75
Outputs:
- result: float32 [4, 2048, 2048], P('shard', 'replica')
- grad_hidden: float32 [4, 2048, 2048], P('shard', 'replica')
- grad_query_weight: float32 [2048, 2048], P('shard')
- grad_key_weight: float32 [2048, 2048], P('shard')
- grad_value_weight: float32 [2048, 2048], P('shard')
- grad_output_weight: float32 [2048, 2048], P('shard')
- grad_gate_weight: float32 [2048, 8192], P('shard')
- grad_up_weight: float32 [2048, 8192], P('shard')
- grad_down_weight: float32 [8192, 2048], P('shard')
- grad_query_gain: float32 [2048], P('shard')
- grad_key_gain: float32 [2048], P('shard')
- grad_attention_gain: float32 [2048], P('shard')
- grad_feed_gain: float32 [2048], P('shard')
- stats: float32 [3], replicated
Inputs may be any that keep to these rules, and one draw needn't show every extreme that they name: `piece_index`: -1 marks text. A picture piece is an aligned run of 256 tokens of one sequence, all holding that run's index within the sequence; the first run of every sequence is text and the last run of every sequence is a picture piece. `pad_flags`: each sequence ends in a run of one or more padded tokens and has none elsewhere.
All inputs are finite; a program needn't handle non-finite values.
Results may differ from a plain program's by a relative error of at most 0.025.
Values may be sent and summed in bfloat16 or wider, within the bound.
No kernel may reach another device: no remote copies, remote signals or barrier semaphores. Data moves between devices by JAX's collectives and lax.ppermute only.
A program may use at most 576 MiB of HBM per device.

v0:
```python
import math
import jax
import jax.numpy as jnp
from jax import lax
from jax.sharding import PartitionSpec as P

HEADS = 16
HEAD = 128
epsilon = 1e-06
theta_base = 500000.0
masked_score = -1e30


def norm_rows(values, gain):
    scaled = values * lax.rsqrt(jnp.mean(values * values, axis=-1, keepdims=True) + epsilon)
    return scaled * gain


def angle_table(positions):
    half_head = HEAD // 2
    rates = theta_base ** (-jnp.arange(half_head).astype(jnp.float32) * (2.0 / HEAD))
    angles = positions.astype(jnp.float32)[:, None] * rates[None, :]
    return (jnp.cos(angles), jnp.sin(angles))


def rotate(values, cosine, sine):
    half_head = HEAD // 2
    first_half = values[..., :half_head]
    second_half = values[..., half_head:]
    cos_wide = cosine[:, None, :]
    sin_wide = sine[:, None, :]
    return jnp.concatenate(
        [
            first_half * cos_wide - second_half * sin_wide,
            second_half * cos_wide + first_half * sin_wide,
        ],
        axis=-1,
    )


def turn_heads(flat_rows, gain, cosine, sine):
    rows_here = flat_rows.shape[0]
    normed = norm_rows(flat_rows, gain).reshape(rows_here, HEADS, HEAD)
    return rotate(normed, cosine, sine).reshape(rows_here, HEADS * HEAD)


def contract_rows(left, right):
    return lax.dot_general(
        left, right, (((0,), (0,)), ((), ())), preferred_element_type=jnp.float32
    )


def contract_cols(left, right):
    return lax.dot_general(
        left, right, (((1,), (1,)), ((), ())), preferred_element_type=jnp.float32
    )


def block_scores(queries, keys_part, info_part, query_place, query_piece, start_key):
    rows_here = queries.shape[0]
    block_rows = keys_part.shape[0]
    scores = jnp.einsum(
        "qhd,khd->hqk",
        queries.reshape(rows_here, HEADS, HEAD),
        keys_part.reshape(block_rows, HEADS, HEAD),
        preferred_element_type=jnp.float32,
    ) * HEAD ** (-0.5)
    key_place = start_key + jnp.arange(block_rows, dtype=jnp.int32)
    key_piece = info_part.astype(jnp.float32)
    allowed = (key_place[None, :] <= query_place[:, None]) | (query_piece[:, None] >= 0.0) & (
        query_piece[:, None] == key_piece[None, :]
    )
    allowed = allowed & (key_piece[None, :] > -1.5)
    return jnp.where(allowed[None], scores, masked_score)


def per_device(
    hidden_in,
    piece_index,
    pad_flags,
    cotangent,
    query_weight,
    key_weight,
    value_weight,
    output_weight,
    gate_weight,
    up_weight,
    down_weight,
    query_gain,
    key_gain,
    attention_gain,
    feed_gain,
):
    tokens = hidden_in[0]
    rows_here = tokens.shape[0]
    width_all = tokens.shape[1]
    hidden_all = gate_weight.shape[1]
    seq_len = rows_here * lax.axis_size("replica")
    first_row = lax.axis_index("replica") * rows_here
    positions = first_row + jnp.arange(rows_here, dtype=jnp.int32)
    cosine, sine = angle_table(positions)
    score_scale = HEAD ** (-0.5)
    input_whole = ()
    feed_whole = ()
    start = jnp.int32(0)
    whole_in = input_whole
    piece_query = lax.all_gather(query_weight, "shard", axis=0, tiled=True)
    piece_key = lax.all_gather(key_weight, "shard", axis=0, tiled=True)
    piece_value = lax.all_gather(value_weight, "shard", axis=0, tiled=True)
    piece_out = lax.all_gather(output_weight, "shard", axis=0, tiled=True)
    gain_one = lax.all_gather(query_gain, "shard", axis=0, tiled=True)
    gain_two = lax.all_gather(key_gain, "shard", axis=0, tiled=True)
    gain_three = lax.all_gather(attention_gain, "shard", axis=0, tiled=True)
    gain_four = lax.all_gather(feed_gain, "shard", axis=0, tiled=True)
    columns = tokens
    sums = tuple(
        (
            jnp.dot(columns, piece, preferred_element_type=jnp.float32)
            for piece in (piece_query, piece_key, piece_value)
        )
    )
    stacked = jnp.stack([gain_one, gain_two, gain_three, gain_four])
    gain_rows = stacked
    whole_in = tuple(
        (
            lax.dynamic_update_slice_in_dim(whole, piece, start, 0)
            for whole, piece in zip(whole_in, (piece_query, piece_key, piece_value))
        )
    )
    (query_raw, key_raw, value_raw), out_whole, gain_rows, input_whole = (
        sums,
        piece_out,
        gain_rows,
        whole_in,
    )
    gains_wide = gain_rows.astype(jnp.float32)

    def turn_local(raw_rows, gain):
        return turn_heads(raw_rows, gain, cosine, sine)

    query_turned, query_pull = jax.vjp(turn_local, query_raw, gains_wide[0])
    key_turned, key_pull = jax.vjp(turn_local, key_raw, gains_wide[1])
    query_low = query_turned.astype(jnp.bfloat16)
    key_low = key_turned.astype(jnp.bfloat16)
    value_low = value_raw.astype(jnp.bfloat16)
    key_info = jnp.where(pad_flags[0] > 0, -2, piece_index[0]).astype(jnp.bfloat16)
    keys_all, values_all, info_all = (
        lax.all_gather(key_low, "replica", axis=0, tiled=True),
        lax.all_gather(value_low, "replica", axis=0, tiled=True),
        lax.all_gather(key_info, "replica", axis=0, tiled=True),
    )
    query_piece = piece_index[0].astype(jnp.float32)
    block_rows = math.gcd(seq_len, 512)
    block_count = seq_len // block_rows

    def scores_at(index):
        start_key = index * block_rows
        keys_part = lax.dynamic_slice_in_dim(keys_all, start_key, block_rows, 0)
        info_part = lax.dynamic_slice_in_dim(info_all, start_key, block_rows, 0)
        return block_scores(query_low, keys_part, info_part, positions, query_piece, start_key)

    def bound_step(index, carried):
        highest, summed = carried
        scores = scores_at(index)
        raised = jnp.maximum(highest, jnp.max(scores, axis=-1))
        summed = summed * jnp.exp(highest - raised) + jnp.sum(
            jnp.exp(scores - raised[..., None]), axis=-1
        )
        return (raised, summed)

    highest, summed = lax.fori_loop(
        0,
        block_count,
        bound_step,
        (
            jnp.full((HEADS, rows_here), masked_score, jnp.float32),
            jnp.zeros((HEADS, rows_here), jnp.float32),
        ),
    )
    log_total = highest + jnp.log(summed)

    def value_step(index, carried):
        start_key = index * block_rows
        weights_low = jnp.exp(scores_at(index) - log_total[..., None]).astype(jnp.bfloat16)
        values_part = lax.dynamic_slice_in_dim(values_all, start_key, block_rows, 0).reshape(
            block_rows, HEADS, HEAD
        )
        return carried + jnp.einsum(
            "hqk,khd->qhd", weights_low, values_part, preferred_element_type=jnp.float32
        )

    mixed = lax.fori_loop(
        0, block_count, value_step, jnp.zeros((rows_here, HEADS, HEAD), jnp.float32)
    )
    attended_low = mixed.reshape(rows_here, width_all).astype(jnp.bfloat16)
    branch_attn = jnp.dot(attended_low, out_whole, preferred_element_type=jnp.float32)
    normed_attn, attn_pull = jax.vjp(norm_rows, branch_attn, gains_wide[2])
    residual = tokens.astype(jnp.float32) + normed_attn
    residual_low = residual.astype(jnp.bfloat16)
    pieces = (
        lax.all_gather(gate_weight, "shard", axis=0, tiled=True),
        lax.all_gather(up_weight, "shard", axis=0, tiled=True),
    )
    start = jnp.int32(0)
    whole_list = feed_whole
    columns = residual_low
    sums = tuple((jnp.dot(columns, piece, preferred_element_type=jnp.float32) for piece in pieces))
    whole_list = tuple(
        (
            lax.dynamic_update_slice_in_dim(whole, piece, start, 0)
            for whole, piece in zip(whole_list, pieces)
        )
    )
    (gate_sum, up_sum), feed_whole = (sums, whole_list)

    def activate(gate_values, up_values):
        return jax.nn.silu(gate_values) * up_values

    activated, act_pull = jax.vjp(activate, gate_sum, up_sum)
    activated_low = activated.astype(jnp.bfloat16)
    piece = lax.all_gather(down_weight, "shard", axis=0, tiled=True)
    columns = activated_low
    partial_sum = jnp.dot(columns, piece, preferred_element_type=jnp.float32)
    normed_feed, feed_pull = jax.vjp(norm_rows, partial_sum, gains_wide[3])
    result = residual + normed_feed
    grad_out = cotangent[0].astype(jnp.float32)
    grad_feed, grad_feed_gain = feed_pull(grad_out)
    grad_feed_low = grad_feed.astype(jnp.bfloat16)
    grad_act = contract_cols(
        grad_feed_low, lax.all_gather(down_weight, "shard", axis=0, tiled=True)
    )
    down_share = lax.psum_scatter(
        contract_rows(activated_low, grad_feed_low).astype(jnp.bfloat16),
        "shard",
        scatter_dimension=0,
        tiled=True,
    ).astype(jnp.float32)
    grad_gate, grad_up = act_pull(grad_act)
    grad_gate_low = grad_gate.astype(jnp.bfloat16)
    grad_up_low = grad_up.astype(jnp.bfloat16)
    pieces = (
        lax.all_gather(gate_weight, "shard", axis=0, tiled=True),
        lax.all_gather(up_weight, "shard", axis=0, tiled=True),
    )
    part_sum = contract_cols(grad_gate_low, pieces[0]) + contract_cols(grad_up_low, pieces[1])
    grad_feed_in = part_sum
    grad_both = jnp.concatenate([grad_gate_low, grad_up_low], axis=1)
    feed_share = lax.psum_scatter(
        contract_rows(residual_low, grad_both).astype(jnp.bfloat16),
        "shard",
        scatter_dimension=0,
        tiled=True,
    ).astype(jnp.float32)
    grad_resid = grad_out + grad_feed_in
    grad_branch, grad_attention_gain = attn_pull(grad_resid)
    grad_branch_low = grad_branch.astype(jnp.bfloat16)
    grad_attended = contract_cols(
        grad_branch_low, lax.all_gather(output_weight, "shard", axis=0, tiled=True)
    )
    grad_mixed = grad_attended.astype(jnp.bfloat16).reshape(rows_here, HEADS, HEAD)
    delta = jnp.einsum("qhd,qhd->hq", grad_mixed.astype(jnp.float32), mixed)
    query_heads = query_low.reshape(rows_here, HEADS, HEAD)

    def back_step(index, carried):
        grad_query, grad_keys, grad_values = carried
        start_key = index * block_rows
        probs = jnp.exp(scores_at(index) - log_total[..., None])
        keys_part = lax.dynamic_slice_in_dim(keys_all, start_key, block_rows, 0).reshape(
            block_rows, HEADS, HEAD
        )
        values_part = lax.dynamic_slice_in_dim(values_all, start_key, block_rows, 0).reshape(
            block_rows, HEADS, HEAD
        )
        value_share = jnp.einsum(
            "hqk,qhd->khd",
            probs.astype(jnp.bfloat16),
            grad_mixed,
            preferred_element_type=jnp.float32,
        )
        grad_probs = jnp.einsum(
            "qhd,khd->hqk", grad_mixed, values_part, preferred_element_type=jnp.float32
        )
        grad_scores = (probs * (grad_probs - delta[..., None])).astype(jnp.bfloat16)
        grad_query = grad_query + jnp.einsum(
            "hqk,khd->qhd", grad_scores, keys_part, preferred_element_type=jnp.float32
        )
        key_share = (
            jnp.einsum("hqk,qhd->khd", grad_scores, query_heads, preferred_element_type=jnp.float32)
            * score_scale
        )
        grad_keys = lax.dynamic_update_slice_in_dim(
            grad_keys, key_share.reshape(block_rows, width_all), start_key, 0
        )
        grad_values = lax.dynamic_update_slice_in_dim(
            grad_values, value_share.reshape(block_rows, width_all), start_key, 0
        )
        return (grad_query, grad_keys, grad_values)

    zero_keys = jnp.zeros((seq_len, width_all), jnp.float32)
    grad_query, grad_keys, grad_values = lax.fori_loop(
        0,
        block_count,
        back_step,
        (jnp.zeros((rows_here, HEADS, HEAD), jnp.float32), zero_keys, zero_keys),
    )
    key_sum, value_sum = (
        lax.psum_scatter(
            grad_keys.astype(jnp.bfloat16), "replica", scatter_dimension=0, tiled=True
        ).astype(jnp.float32),
        lax.psum_scatter(
            grad_values.astype(jnp.bfloat16), "replica", scatter_dimension=0, tiled=True
        ).astype(jnp.float32),
    )
    grad_query_raw, grad_query_gain = query_pull(
        (grad_query * score_scale).reshape(rows_here, width_all)
    )
    grad_key_raw, grad_key_gain = key_pull(key_sum)
    query_back_low = grad_query_raw.astype(jnp.bfloat16)
    key_back_low = grad_key_raw.astype(jnp.bfloat16)
    value_back_low = value_sum.astype(jnp.bfloat16)
    pieces = (
        lax.all_gather(query_weight, "shard", axis=0, tiled=True),
        lax.all_gather(key_weight, "shard", axis=0, tiled=True),
        lax.all_gather(value_weight, "shard", axis=0, tiled=True),
    )
    part_sum = (
        contract_cols(query_back_low, pieces[0])
        + contract_cols(key_back_low, pieces[1])
        + contract_cols(value_back_low, pieces[2])
    )
    grad_tokens = grad_resid + part_sum
    grad_inputs = jnp.concatenate([query_back_low, key_back_low, value_back_low], axis=1)
    input_share = lax.psum_scatter(
        jnp.concatenate(
            [contract_rows(tokens, grad_inputs), contract_rows(attended_low, grad_branch_low)],
            axis=1,
        ).astype(jnp.bfloat16),
        "shard",
        scatter_dimension=0,
        tiled=True,
    ).astype(jnp.float32)
    input_share, feed_share, down_share = (
        lax.psum(input_share.astype(jnp.bfloat16), "replica").astype(jnp.float32),
        lax.psum(feed_share.astype(jnp.bfloat16), "replica").astype(jnp.float32),
        lax.psum(down_share.astype(jnp.bfloat16), "replica").astype(jnp.float32),
    )
    valid = (pad_flags[0] == 0).astype(jnp.float32)[:, None]
    stat_terms = jnp.stack(
        [
            jnp.sum(valid * result * result),
            jnp.sum(valid * branch_attn * branch_attn),
            jnp.sum(valid * partial_sum * partial_sum),
            jnp.sum(valid),
        ]
    )
    gain_terms = jnp.stack([grad_query_gain, grad_key_gain, grad_attention_gain, grad_feed_gain])
    gain_terms, stat_terms = lax.psum((gain_terms, stat_terms), ("replica", "shard"))
    gain_width = query_gain.shape[0]
    gain_mine = lax.dynamic_slice_in_dim(
        gain_terms, lax.axis_index("shard") * gain_width, gain_width, 1
    )
    stats = jnp.sqrt(stat_terms[:3] / (stat_terms[3] * width_all))
    return (
        result[None],
        grad_tokens[None],
        input_share[:, :width_all],
        input_share[:, width_all : 2 * width_all],
        input_share[:, 2 * width_all : 3 * width_all],
        input_share[:, 3 * width_all :],
        feed_share[:, :hidden_all],
        feed_share[:, hidden_all:],
        down_share,
        gain_mine[0],
        gain_mine[1],
        gain_mine[2],
        gain_mine[3],
        stats,
    )


def solution(mesh):
    placed = (
        P("shard", "replica", None),
        P("shard", "replica"),
        P("shard", "replica"),
        P("shard", "replica", None),
        P("shard", None),
        P("shard", None),
        P("shard", None),
        P("shard", None),
        P("shard", None),
        P("shard", None),
        P("shard", None),
        P("shard"),
        P("shard"),
        P("shard"),
        P("shard"),
    )
    return jax.shard_map(
        per_device,
        mesh=mesh,
        in_specs=placed,
        out_specs=(
            P("shard", "replica", None),
            P("shard", "replica", None),
            P("shard", None),
            P("shard", None),
            P("shard", None),
            P("shard", None),
            P("shard", None),
            P("shard", None),
            P("shard", None),
            P("shard"),
            P("shard"),
            P("shard"),
            P("shard"),
            P(),
        ),
        check_vma=False,
    )
```

profile of v0, /device:TPU:0, one launch (start us, length us, event | category | flops | bytes accessed | tf_op | source)
XLA Modules:
  0.0 3683.2 jit_solution(10131605898892978450)
XLA Ops:
  9.5 90.7 %all-gather.15.cloned.1.call-done = bf16[2048,2048]{1,0:T(8,128)(2,1)} async-done(((bf16[512,2048]{1,0:T(8,128)(2,1)}), bf16[2048,2048]{1,0:T(8,128)(2,1)}) %all-gather.15.cloned.1.call-update) | async-done | bytes 8388624 | tf_op jit(solution)/shard_map/all_gather | solution.py:109
  138.4 51.5 %all-gather.19.cloned.1.call-done = bf16[2048,2048]{1,0:T(8,128)(2,1)} async-done(((bf16[512,2048]{1,0:T(8,128)(2,1)}), bf16[2048,2048]{1,0:T(8,128)(2,1)}) %all-gather.19.cloned.1.call-update) | async-done | bytes 8388624 | tf_op jit(solution)/shard_map/all_gather | solution.py:108
  205.4 11.7 all-gather
  217.7 61.7 %all-gather.23.cloned.1.call-done = bf16[2048,2048]{1,0:T(8,128)(2,1)} async-done(((bf16[512,2048]{1,0:T(8,128)(2,1)}), bf16[2048,2048]{1,0:T(8,128)(2,1)}) %all-gather.23.cloned.1.call-update) | async-done | bytes 8388624 | tf_op jit(solution)/shard_map/all_gather | solution.py:107
  291.6 71.9 %all-gather.17.cloned.1.call-done = bf16[2048,2048]{1,0:T(8,128)(2,1)} async-done(((bf16[256,2048]{1,0:T(8,128)(2,1)}), bf16[2048,2048]{1,0:T(8,128)(2,1)}) %all-gather.17.cloned.1.call-update) | async-done | bytes 8388624 | tf_op jit(solution)/shard_map/all_gather | solution.py:149
  363.5 12.3 copy.126
  375.9 70.7 %all-gather.21.cloned.1.call-done = bf16[2048,2048]{0,1:T(8,128)(2,1)} async-done(((bf16[256,2048]{0,1:T(8,128)(2,1)}), bf16[2048,2048]{0,1:T(8,128)(2,1)}) %all-gather.21.cloned.1.call-update) | async-done | bytes 8388624 | tf_op jit(solution)/shard_map/all_gather | solution.py:148
  446.6 51.6 %while.48 = (s32[]{:T(128)}, f32[16,256]{1,0:T(8,128)S(1)}, f32[16,256]{1,0:T(8,128)S(1)}, f32[256]{0:T(256)S(1)}, bf16[2048]{0:T(1024)(128)(2,1)S(1)}, /*index=...) while((s32[]{:T(128)}, f32[16,256]{1,0:T(8,128)S(1)}, ...), condition=%wide.region_5.6_spmd.clone, body=%wide.region_2.5_spmd.clone.sunk | while | flops 552229376 | bytes 24739520 | solution.py:171
  498.2 42.5 %while.49 = (s32[]{:T(128)}, f32[256,16,128]{0,2,1:T(8,128)}, bf16[2048,2048]{0,1:T(8,128)(2,1)}, f32[256]{0:T(256)S(1)}, bf16[2048]{0:T(1024)(128)(2,1)S(1)}, /...) while((s32[]{:T(128)}, f32[256,16,128]{0,2,1:T(8,128)}, ...), condition=%wide.region_7.8_spmd.clone, body=%wide.region_6.7_spmd.clone.sunk | while | flops 1083836928 | bytes 18120392 | solution.py:192
  554.1 279.1 %all-gather.27.cloned.1.call-done = bf16[2048,8192]{1,0:T(8,128)(2,1)} async-done(((bf16[512,8192]{1,0:T(8,128)(2,1)}), bf16[2048,8192]{1,0:T(8,128)(2,1)}) %all-gather.27.cloned.1.call-update) | async-done | bytes 33554448 | tf_op jit(solution)/shard_map/all_gather | solution.py:201
  833.2 22.2 fusion.92
  855.5 276.8 %all-gather.29.cloned.1.call-done = bf16[2048,8192]{1,0:T(8,128)(2,1)} async-done(((bf16[512,8192]{1,0:T(8,128)(2,1)}), bf16[2048,8192]{1,0:T(8,128)(2,1)}) %all-gather.29.cloned.1.call-update) | async-done | bytes 33554448 | tf_op jit(solution)/shard_map/all_gather | solution.py:202
  1132.3 26.9 multiply_convert_fusion.1
  1159.2 272.2 %all-gather.31.cloned.1.call-done = bf16[8192,2048]{1,0:T(8,128)(2,1)} async-done(((bf16[2048,2048]{1,0:T(8,128)(2,1)}), bf16[8192,2048]{1,0:T(8,128)(2,1)}) %all-gather.31.cloned.1.call-update) | async-done | bytes 33554448 | tf_op jit(solution)/shard_map/all_gather | solution.py:221
  1431.4 16.6 multiply_reduce_fusion.7
  1450.1 22.0 multiply_convert_fusion
  1472.1 17.1 fusion.93
  1489.2 20.5 multiply_reduce_fusion.1
  1531.4 106.4 %while.50 = (s32[]{:T(128)}, f32[256,16,128]{0,2,1:T(8,128)}, bf16[2048,2048]{0,1:T(8,128)(2,1)}, bf16[2048,2048]{1,0:T(8,128)(2,1)}, bf16[2048,2048]{0,1:T(8,12...) while((s32[]{:T(128)}, f32[256,16,128]{0,2,1:T(8,128)}, ...), condition=%wide.region_13.14_spmd.clone, body=%wide.region_12.13_spmd.clone.sunk | while | flops 2709129728 | bytes 103219016 | solution.py:300
  1639.7 16.4 convolution_convert_fusion.1
  1665.9 61.8 %reduce-scatter.10.cloned.1.call-done = bf16[256,2048]{0,1:T(8,128)(2,1)} async-done(((bf16[2048,2048]{0,1:T(8,128)(2,1)}), bf16[256,2048]{0,1:T(8,128)(2,1)}) %reduce-scatter.10.cloned.1.call-update) | async-done | bytes 1048592 | tf_op jit(solution)/shard_map/reduce_scatter | solution.py:307
  1741.6 76.9 %reduce-scatter.12.cloned.1.call-done = bf16[256,2048]{1,0:T(8,128)(2,1)} async-done(((bf16[2048,2048]{1,0:T(8,128)(2,1)}), bf16[256,2048]{1,0:T(8,128)(2,1)}) %reduce-scatter.12.cloned.1.call-update) | async-done | bytes 1048592 | tf_op jit(solution)/shard_map/reduce_scatter | solution.py:310
  1818.5 13.4 convert_bitcast_fusion
  1831.8 24.4 pad_maximum_fusion
  1857.4 29.1 convolution_convert_fusion
  1886.8 221.6 %reduce-scatter.18.cloned.1.call-done = bf16[2048,2048]{1,0:T(8,128)(2,1)} async-done(((bf16[8192,2048]{1,0:T(8,128)(2,1)}), bf16[2048,2048]{1,0:T(8,128)(2,1)}) %reduce-scatter.18.cloned.1.call-update) | async-done | bytes 8388624
  2108.4 292.0 %reduce-scatter.14.cloned.1.call-done = bf16[512,8192]{0,1:T(8,128)(2,1)} async-done(((bf16[2048,8192]{0,1:T(8,128)(2,1)}), bf16[512,8192]{0,1:T(8,128)(2,1)}) %reduce-scatter.14.cloned.1.call-update) | async-done | bytes 8388624 | tf_op jit(solution)/shard_map/reduce_scatter | solution.py:333
  2400.5 561.2 %reduce-scatter.16.cloned.1.call-done = bf16[512,16384]{1,0:T(8,128)(2,1)} async-done(((bf16[2048,16384]{1,0:T(8,128)(2,1)}), bf16[512,16384]{1,0:T(8,128)(2,1)}) %reduce-scatter.16.cloned.1.call-update) | async-done | bytes 16777232
  2965.6 41.1 %all-reduce.6 = (f32[4,2048]{1,0:T(4,128)S(1)}, f32[4]{0:T(128)S(1)}) all-reduce(f32[4,2048]{1,0:T(4,128)S(1)} %pad_maximum_fusion.2, f32[4]{0:T(128)S(1)} %pad_maximum_fusion.3), channel_id=1, replica_groups=mesh['replica'=8,'shard'=4] {'replica','shard'}, use_global_device_ids=true, to_apply=%region_28.29 | all-reduce | flops 8196 | bytes 65568 | tf_op jit(solution)/shard_map/psum | solution.py:357
  3025.0 591.2 %all-reduce.10.cloned.1.call-done = (bf16[512,8192]{0,1:T(8,128)(2,1)}, bf16[512,16384]{1,0:T(8,128)(2,1)}, bf16[2048,2048]{1,0:T(8,128)(2,1)}) async-done(((bf16[512,8192]{0,1:T(8,128)(2,1)}, bf16[512,16384]{1,0:T(8,128)(2,1)}, bf16[2048,2048]{1,0:T(8,128)(2,1)}), (bf16[512,8192]{0,1:T(8,128)(2,1)}, bf16[512,16384]{1,0:T(8,128)(2,1)}, bf16[2048,2048]{1,0:T(8,128)(2,1)})) %all-reduce.10.cloned.1.call-update) | async-done | bytes 33554448 | tf_op jit(solution)/shard_map/psum | solution.py:343
  3616.1 16.9 fusion.86
  3664.8 11.7 convert_element_type.207
  (412 shorter events, 384.8 us)
Async XLA Ops:
  7.2 93.0 %all-gather.15.cloned.1.call-start = ((), (), s32[]{:S(2)}) async-start(), calls=%async_computation.5 | async-start | bytes 10485760 | tf_op jit(solution)/shard_map/all_gather | solution.py:109
  7.9 92.3 %copy-start.22 = (bf16[1,256,2048]{2,1,0:T(8,128)(2,1)S(1)}, bf16[1,256,2048]{2,1,0:T(8,128)(2,1)}, u32[]{:S(2)}) copy-start(bf16[1,256,2048]{2,1,0:T(8,128)(2,1)} %param.21) | copy-start | bytes 3145732
  7.9 181.9 %all-gather.19.cloned.1.call-start = ((), (), s32[]{:S(2)}) async-start(), calls=%async_computation.7 | async-start | bytes 10485760 | tf_op jit(solution)/shard_map/all_gather | solution.py:108
  8.7 270.7 %all-gather.23.cloned.1.call-start = ((), (), s32[]{:S(2)}) async-start(), calls=%async_computation.9 | async-start | bytes 10485760 | tf_op jit(solution)/shard_map/all_gather | solution.py:107
  9.4 97.6 %copy-start.62 = (bf16[512]{0:T(512)(128)(2,1)S(1)}, bf16[512]{0:T(512)(128)(2,1)}, u32[]{:S(2)}) copy-start(bf16[512]{0:T(512)(128)(2,1)} %param.32) | copy-start | bytes 3076
  9.4 97.6 %copy-start.63 = (bf16[512]{0:T(512)(128)(2,1)S(1)}, bf16[512]{0:T(512)(128)(2,1)}, u32[]{:S(2)}) copy-start(bf16[512]{0:T(512)(128)(2,1)} %param.33) | copy-start | bytes 3076
  9.4 97.6 %copy-start.64 = (bf16[512]{0:T(512)(128)(2,1)S(1)}, bf16[512]{0:T(512)(128)(2,1)}, u32[]{:S(2)}) copy-start(bf16[512]{0:T(512)(128)(2,1)} %param.34) | copy-start | bytes 3076
  9.4 97.6 %copy-start.65 = (bf16[512]{0:T(512)(128)(2,1)S(1)}, bf16[512]{0:T(512)(128)(2,1)}, u32[]{:S(2)}) copy-start(bf16[512]{0:T(512)(128)(2,1)} %param.35) | copy-start | bytes 3076
  9.4 354.1 %all-gather.17.cloned.1.call-start = ((), (), s32[]{:S(2)}) async-start(), calls=%async_computation.6 | async-start | bytes 9437184 | tf_op jit(solution)/shard_map/all_gather | solution.py:149
  106.9 339.7 %all-gather.21.cloned.1.call-start = ((), (), s32[]{:S(2)}) async-start(), calls=%async_computation.8 | async-start | bytes 9437184 | tf_op jit(solution)/shard_map/all_gather | solution.py:148
  137.7 151.1 %copy-start.30 = (f32[256,64]{0,1:T(8,128)}, f32[256,64]{0,1:T(8,128)S(1)}, u32[]{:S(2)}) copy-start(f32[256,64]{0,1:T(8,128)S(1)} %get-tuple-element.949) | copy-start | bytes 196612
  137.7 151.1 %copy-start.32 = (f32[256,64]{0,1:T(8,128)}, f32[256,64]{0,1:T(8,128)S(1)}, u32[]{:S(2)}) copy-start(f32[256,64]{0,1:T(8,128)S(1)} %get-tuple-element.950) | copy-start | bytes 196612
  138.4 57.3 %copy-start.42 = (f32[1,2048]{1,0:T(1,128)}, f32[1,2048]{1,0:T(1,128)S(1)}, u32[]{:S(2)}) copy-start(f32[1,2048]{1,0:T(1,128)S(1)} %get-tuple-element.948) | copy-start | bytes 24580
  138.4 147.4 %copy-start.40 = (f32[1,2048]{1,0:T(1,128)}, f32[1,2048]{1,0:T(1,128)S(1)}, u32[]{:S(2)}) copy-start(f32[1,2048]{1,0:T(1,128)S(1)} %get-tuple-element.947) | copy-start | bytes 24580
  202.4 340.7 %all-gather.25.cloned.1.call-start = ((), (), s32[]{:S(2)}) async-start(), calls=%async_computation.10 | async-start | bytes 10485760 | tf_op jit(solution)/shard_map/all_gather | solution.py:110
  203.0 630.2 %all-gather.27.cloned.1.call-start = ((), (), s32[]{:S(2)}) async-start(), calls=%async_computation.11 | async-start | bytes 41943040 | tf_op jit(solution)/shard_map/all_gather | solution.py:201
  203.8 928.5 %all-gather.29.cloned.1.call-start = ((), (), s32[]{:S(2)}) async-start(), calls=%async_computation.12 | async-start | bytes 41943040 | tf_op jit(solution)/shard_map/all_gather | solution.py:202
  204.5 1226.8 %all-gather.31.cloned.1.call-start = ((), (), s32[]{:S(2)}) async-start(), calls=%async_computation.13 | async-start | bytes 41943040 | tf_op jit(solution)/shard_map/all_gather | solution.py:221
  205.3 1522.3 %reduce-scatter.10.cloned.1.call-start = ((), (), s32[]{:S(2)}) async-start(), calls=%async_computation.14 | async-start | bytes 9437184 | tf_op jit(solution)/shard_map/reduce_scatter | solution.py:307
  291.0 84.9 %copy-start.4 = (bf16[256,16,128]{0,2,1:T(8,128)(2,1)}, bf16[256,16,128]{0,2,1:T(8,128)(2,1)S(1)}, u32[]{:S(2)}) copy-start(bf16[256,16,128]{0,2,1:T(8,128)(2,1)S(1)} %maximum_convert_fusion) | copy-start | bytes 3145732
  554.1 578.2 %copy-start.20 = (bf16[256,2048]{1,0:T(8,128)(2,1)}, bf16[256,2048]{1,0:T(8,128)(2,1)S(1)}, u32[]{:S(2)}) copy-start(bf16[256,2048]{1,0:T(8,128)(2,1)S(1)} %fusion.71) | copy-start | bytes 3145732
  1448.0 24.1 copy-start.16
  1472.1 39.6 %slice-start = ((s8[8388608]{0:T(1024)(128)(4,1)}), s8[4194304]{0:T(1024)(128)(4,1)S(1)}, s32[]{:S(2)}) async-start(s8[8388608]{0:T(1024)(128)(4,1)} %bitcast.255), calls=%async_computation.20 | async-start | bytes 8388608
  1637.8 180.7 %reduce-scatter.12.cloned.1.call-start = ((), (), s32[]{:S(2)}) async-start(), calls=%async_computation.15 | async-start | bytes 9437184 | tf_op jit(solution)/shard_map/reduce_scatter | solution.py:310
  1638.6 469.9 %reduce-scatter.18.cloned.1.call-start = ((), (), s32[]{:S(2)}) async-start(), calls=%async_computation.18 | async-start | bytes 41943040
  1656.2 744.3 %reduce-scatter.14.cloned.1.call-start = ((), (), s32[]{:S(2)}) async-start(), calls=%async_computation.16 | async-start | bytes 41943040 | tf_op jit(solution)/shard_map/reduce_scatter | solution.py:333
  1665.8 63.2 %copy-start.19 = (f32[256,16,128]{0,2,1:T(8,128)S(1)}, f32[256,16,128]{0,2,1:T(8,128)}, u32[]{:S(2)}) copy-start(f32[256,16,128]{0,2,1:T(8,128)} %broadcast_multiply_fusion) | copy-start | bytes 6291460
  1665.8 63.2 %copy-start.31 = (f32[256,64]{0,1:T(8,128)S(1)}, f32[256,64]{0,1:T(8,128)}, u32[]{:S(2)}) copy-start(f32[256,64]{0,1:T(8,128)} %copy-done.30) | copy-start | bytes 196612
  1665.8 63.2 %copy-start.33 = (f32[256,64]{0,1:T(8,128)S(1)}, f32[256,64]{0,1:T(8,128)}, u32[]{:S(2)}) copy-start(f32[256,64]{0,1:T(8,128)} %copy-done.32) | copy-start | bytes 196612
  1741.1 77.4 %copy-start.24 = (bf16[1,256,2048]{2,1,0:T(8,128)(2,1)S(1)}, bf16[1,256,2048]{2,1,0:T(8,128)(2,1)}, u32[]{:S(2)}) copy-start(bf16[1,256,2048]{2,1,0:T(8,128)(2,1)} %param.21) | copy-start | bytes 3145732
  1856.3 1105.4 %reduce-scatter.16.cloned.1.call-start = ((), (), s32[]{:S(2)}) async-start(), calls=%async_computation.17 | async-start | bytes 83886080
  1886.5 1729.6 %all-reduce.10.cloned.1.call-start = ((), (), s32[]{:S(2)}) async-start(), calls=%async_computation.19 | async-start | bytes 67108864 | tf_op jit(solution)/shard_map/psum | solution.py:343
  (63 other events, 316.3 us)
Sparse Core Ops, SparseCore 0:
  9.9 90.2 all-gather.14
  102.0 87.7 all-gather.18
  191.7 87.6 all-gather.22
  281.4 82.0 all-gather.16
  365.5 81.0 all-gather.20
  448.3 85.7 all-gather.24
  536.0 297.2 all-gather.26
  835.1 297.2 all-gather.28
  1134.1 297.2 all-gather.30
  1638.0 89.6 reduce-scatter.9
  1730.5 87.9 reduce-scatter.11
  1821.4 286.9 reduce-scatter.17
  2111.8 288.6 reduce-scatter.13
  2403.4 558.2 reduce-scatter.15
  2964.4 651.7 all-reduce.9
where the time goes:
time: 3690 us; the launch traced here: 3680 us
  waiting for transfers between devices  2980 us (81%)
  matrix products  339 us (9%)
  local copies, waits for them, and re-layouts  166 us (4%)
  other arithmetic  92.9 us (3%)
  blocking collectives  83.1 us (2%)
    unnamed x17, waiting for transfers between devices  788 us
    psum x1, waiting for transfers between devices, per_device(): lax.psum(input_share.astype(jnp.bfloat16), 'replica').astype(jnp.float32)  591 us
    reduce_scatter x1, waiting for transfers between devices, per_device(): lax.psum_scatter(jnp.concatenate([contract_rows(tokens, grad_inputs), con...  292 us
    all_gather x1, waiting for transfers between devices, per_device(): lax.all_gather(gate_weight, 'shard', axis=0, tiled=True)  279 us
    all_gather x1, waiting for transfers between devices, per_device(): lax.all_gather(up_weight, 'shard', axis=0, tiled=True)  277 us
    all_gather x1, waiting for transfers between devices, per_device(): piece = lax.all_gather(down_weight, 'shard', axis=0, tiled=True)  272 us
    all_gather x1, waiting for transfers between devices, per_device(): piece_value = lax.all_gather(value_weight, 'shard', axis=0, tiled=True)  90.7 us
    dot_general x7, matrix products, contract_cols(): lax.dot_general(left, right, (((1,), (1,)), ((), ())), preferred_element_...  77.7 us
  transfers between devices with their start and end apart: 15, of which 14 were waited for; matrix products, arithmetic and copies ran while one was open for 9% of the time, Pallas kernels for 0%

commit v1 on v0

--- a/solution.py
+++ b/solution.py
@@ -9,6 +9,12 @@
 epsilon = 1e-06
 theta_base = 500000.0
 masked_score = -1e30
+
+
+def run_the_steps_all(here_x, mat, mesh_ax):
+    passed = jnp.concatenate([here_x, mat], axis=1)
+    carry_out = jax.lax.all_gather(passed, axis_name=mesh_ax, axis=0, tiled=True)
+    return jnp.split(carry_out, [here_x.shape[1]], axis=1)
 
 
 def norm_rows(values, gain):
@@ -105,8 +111,7 @@
     start = jnp.int32(0)
     whole_in = input_whole
     piece_query = lax.all_gather(query_weight, "shard", axis=0, tiled=True)
-    piece_key = lax.all_gather(key_weight, "shard", axis=0, tiled=True)
-    piece_value = lax.all_gather(value_weight, "shard", axis=0, tiled=True)
+    piece_key, piece_value = run_the_steps_all(key_weight, value_weight, "shard")
     piece_out = lax.all_gather(output_weight, "shard", axis=0, tiled=True)
     gain_one = lax.all_gather(query_gain, "shard", axis=0, tiled=True)
     gain_two = lax.all_gather(key_gain, "shard", axis=0, tiled=True)

time: 3690 us -> 3830 us (1.038)
  waiting for transfers between devices: 2980 us -> 3160 us
  local copies, waits for them, and re-layouts: 166 us -> 124 us
    all_gather x2 -> x3, waiting for transfers between devices: 142 us -> 244 us  [the longest x1 126 us: run_the_steps_all(): jax.lax.all_gather(passed, axis_name=mesh_ax, axis=0, tiled=True)]
    psum x1, waiting for transfers between devices: 591 us -> 645 us  [per_device(): lax.psum(input_share.astype(jnp.bfloat16), 'replica').astype(jnp.float32)]
    all_gather x1, waiting for transfers between devices: 0.02 us -> 41.7 us  [per_device(): piece_out = lax.all_gather(output_weight, 'shard', axis=0, tiled=True)]
    all_gather x1, waiting for transfers between devices: 71.9 us -> 32.1 us  [per_device(): lax.all_gather(value_low, 'replica', axis=0, tiled=True)]
    unnamed x17 -> x18, waiting for transfers between devices: 788 us -> 787 us
  transfers between devices with their start and end apart: 15 -> 16, of which waited for: 14 -> 16; matrix products, arithmetic and copies ran while one was open for 9% -> 8% of each run, Pallas kernels for 0% -> 0%
where the time goes in v1:
time: 3830 us; the launch traced here: 3820 us
  waiting for transfers between devices  3160 us (83%)
  matrix products  342 us (9%)
  local copies, waits for them, and re-layouts  124 us (3%)
  other arithmetic  91.9 us (2%)
  blocking collectives  84.4 us (2%)
    unnamed x18, waiting for transfers between devices  787 us
    psum x1, waiting for transfers between devices, per_device(): lax.psum(input_share.astype(jnp.bfloat16), 'replica').astype(jnp.float32)  645 us
    all_gather x1, waiting for transfers between devices, per_device(): lax.all_gather(gate_weight, 'shard', axis=0, tiled=True)  292 us
    reduce_scatter x1, waiting for transfers between devices, per_device(): lax.psum_scatter(jnp.concatenate([contract_rows(tokens, grad_inputs), con...  292 us
    all_gather x1, waiting for transfers between devices, per_device(): lax.all_gather(up_weight, 'shard', axis=0, tiled=True)  277 us
    all_gather x1, waiting for transfers between devices, per_device(): piece = lax.all_gather(down_weight, 'shard', axis=0, tiled=True)  272 us
    all_gather x1, waiting for transfers between devices, run_the_steps_all(): jax.lax.all_gather(passed, axis_name=mesh_ax, axis=0, tiled=True)  126 us
    dot_general x7, matrix products, contract_cols(): lax.dot_general(left, right, (((1,), (1,)), ((), ())), preferred_element_...  86.8 us
  transfers between devices with their start and end apart: 16, of which 16 were waited for; matrix products, arithmetic and copies ran while one was open for 8% of the time, Pallas kernels for 0%

profile of v1, /device:TPU:0, one launch (start us, length us, event | category | flops | bytes accessed | tf_op | source)
XLA Modules:
  0.0 3820.3 jit_solution(17358808176151524597)
XLA Ops:
  46.7 125.8 %all-gather.16.cloned.1.call-done = bf16[2048,4096]{1,0:T(8,128)(2,1)} async-done(((bf16[512,4096]{1,0:T(8,128)(2,1)}), bf16[2048,4096]{1,0:T(8,128)(2,1)}) %all-gather.16.cloned.1.call-update) | async-done | bytes 16777232 | tf_op jit(solution)/shard_map/all_gather | solution.py:16
  191.8 11.8 all-gather
  204.2 57.7 %all-gather.22.cloned.1.call-done = bf16[2048,2048]{1,0:T(8,128)(2,1)} async-done(((bf16[512,2048]{1,0:T(8,128)(2,1)}), bf16[2048,2048]{1,0:T(8,128)(2,1)}) %all-gather.22.cloned.1.call-update) | async-done | bytes 8388624 | tf_op jit(solution)/shard_map/all_gather | solution.py:113
  273.2 73.5 %all-gather.20.cloned.1.call-done = bf16[2048,2048]{0,1:T(8,128)(2,1)} async-done(((bf16[256,2048]{0,1:T(8,128)(2,1)}), bf16[2048,2048]{0,1:T(8,128)(2,1)}) %all-gather.20.cloned.1.call-update) | async-done | bytes 8388624 | tf_op jit(solution)/shard_map/all_gather | solution.py:153
  346.6 50.6 %while.48 = (s32[]{:T(128)}, f32[16,256]{1,0:T(8,128)S(1)}, f32[16,256]{1,0:T(8,128)S(1)}, f32[256]{0:T(256)S(1)}, bf16[2048]{0:T(1024)(128)(2,1)S(1)}, /*index=...) while((s32[]{:T(128)}, f32[16,256]{1,0:T(8,128)S(1)}, ...), condition=%wide.region_5.6_spmd.clone, body=%wide.region_2.5_spmd.clone.sunk | while | flops 552229376 | bytes 24739520 | solution.py:176
  397.3 32.1 all-gather.18.cloned.1.call-done
  429.4 42.7 %while.49 = (s32[]{:T(128)}, f32[256,16,128]{0,2,1:T(8,128)}, bf16[2048,2048]{0,1:T(8,128)(2,1)}, f32[256]{0:T(256)S(1)}, bf16[2048]{0:T(1024)(128)(2,1)S(1)}, /...) while((s32[]{:T(128)}, f32[256,16,128]{0,2,1:T(8,128)}, ...), condition=%wide.region_7.8_spmd.clone, body=%wide.region_6.7_spmd.clone.sunk | while | flops 1083836928 | bytes 18120392 | solution.py:197
  475.2 41.7 %all-gather.24.cloned.1.call-done = bf16[2048,2048]{1,0:T(8,128)(2,1)} async-done(((bf16[512,2048]{1,0:T(8,128)(2,1)}), bf16[2048,2048]{1,0:T(8,128)(2,1)}) %all-gather.24.cloned.1.call-update) | async-done | bytes 8388624 | tf_op jit(solution)/shard_map/all_gather | solution.py:115
  523.6 292.2 %all-gather.26.cloned.1.call-done = bf16[2048,8192]{1,0:T(8,128)(2,1)} async-done(((bf16[512,8192]{1,0:T(8,128)(2,1)}), bf16[2048,8192]{1,0:T(8,128)(2,1)}) %all-gather.26.cloned.1.call-update) | async-done | bytes 33554448 | tf_op jit(solution)/shard_map/all_gather | solution.py:206
  815.9 22.2 fusion.106
  838.1 276.8 %all-gather.28.cloned.1.call-done = bf16[2048,8192]{1,0:T(8,128)(2,1)} async-done(((bf16[512,8192]{1,0:T(8,128)(2,1)}), bf16[2048,8192]{1,0:T(8,128)(2,1)}) %all-gather.28.cloned.1.call-update) | async-done | bytes 33554448 | tf_op jit(solution)/shard_map/all_gather | solution.py:207
  1114.9 26.9 multiply_convert_fusion.1
  1141.8 272.2 %all-gather.30.cloned.1.call-done = bf16[8192,2048]{1,0:T(8,128)(2,1)} async-done(((bf16[2048,2048]{1,0:T(8,128)(2,1)}), bf16[8192,2048]{1,0:T(8,128)(2,1)}) %all-gather.30.cloned.1.call-update) | async-done | bytes 33554448 | tf_op jit(solution)/shard_map/all_gather | solution.py:226
  1414.0 16.6 multiply_reduce_fusion.5
  1434.0 23.2 multiply_convert_fusion
  1457.2 16.9 fusion.107
  1474.1 21.0 multiply_reduce_fusion.1
  1516.8 80.1 %while.50 = (s32[]{:T(128)}, f32[256,16,128]{0,2,1:T(8,128)}, bf16[2048,2048]{0,1:T(8,128)(2,1)}, bf16[2048,2048]{0,1:T(8,128)(2,1)}, bf16[2048,2048]{0,1:T(8,12...) while((s32[]{:T(128)}, f32[256,16,128]{0,2,1:T(8,128)}, ...), condition=%wide.region_13.14_spmd.clone, body=%wide.region_12.13_spmd.clone.sunk | while | flops 2709129728 | bytes 99024728 | solution.py:305
  1598.9 16.4 convolution_convert_fusion.1
  1624.3 62.5 %reduce-scatter.10.cloned.1.call-done = bf16[256,2048]{0,1:T(8,128)(2,1)} async-done(((bf16[2048,2048]{0,1:T(8,128)(2,1)}), bf16[256,2048]{0,1:T(8,128)(2,1)}) %reduce-scatter.10.cloned.1.call-update) | async-done | bytes 1048592 | tf_op jit(solution)/shard_map/reduce_scatter | solution.py:312
  1693.9 83.6 %reduce-scatter.12.cloned.1.call-done = bf16[256,2048]{0,1:T(8,128)(2,1)} async-done(((bf16[2048,2048]{0,1:T(8,128)(2,1)}), bf16[256,2048]{0,1:T(8,128)(2,1)}) %reduce-scatter.12.cloned.1.call-update) | async-done | bytes 1048592 | tf_op jit(solution)/shard_map/reduce_scatter | solution.py:315
  1777.5 13.3 convert_bitcast_fusion
  1790.8 24.4 pad_maximum_fusion
  1816.4 29.1 convolution_convert_fusion
  1847.0 220.6 %reduce-scatter.18.cloned.1.call-done = bf16[2048,2048]{1,0:T(8,128)(2,1)} async-done(((bf16[8192,2048]{1,0:T(8,128)(2,1)}), bf16[2048,2048]{1,0:T(8,128)(2,1)}) %reduce-scatter.18.cloned.1.call-update) | async-done | bytes 8388624
  2067.6 291.9 %reduce-scatter.14.cloned.1.call-done = bf16[512,8192]{0,1:T(8,128)(2,1)} async-done(((bf16[2048,8192]{0,1:T(8,128)(2,1)}), bf16[512,8192]{0,1:T(8,128)(2,1)}) %reduce-scatter.14.cloned.1.call-update) | async-done | bytes 8388624 | tf_op jit(solution)/shard_map/reduce_scatter | solution.py:338
  2359.5 561.4 %reduce-scatter.16.cloned.1.call-done = bf16[512,16384]{1,0:T(8,128)(2,1)} async-done(((bf16[2048,16384]{1,0:T(8,128)(2,1)}), bf16[512,16384]{1,0:T(8,128)(2,1)}) %reduce-scatter.16.cloned.1.call-update) | async-done | bytes 16777232
  2924.8 39.9 %all-reduce.6 = (f32[4,2048]{1,0:T(4,128)S(1)}, f32[4]{0:T(128)S(1)}) all-reduce(f32[4,2048]{1,0:T(4,128)S(1)} %pad_maximum_fusion.3, f32[4]{0:T(128)S(1)} %pad_maximum_fusion.4), channel_id=1, replica_groups=mesh['replica'=8,'shard'=4] {'replica','shard'}, use_global_device_ids=true, to_apply=%region_28.29 | all-reduce | flops 8196 | bytes 65568 | tf_op jit(solution)/shard_map/psum | solution.py:362
  2974.2 36.2 all-gather.32.cloned.1.call-done
  3018.1 81.7 %all-gather.34.cloned.1.call-done = bf16[2048,2048]{1,0:T(8,128)(2,1)} async-done(((bf16[512,2048]{1,0:T(8,128)(2,1)}), bf16[2048,2048]{1,0:T(8,128)(2,1)}) %all-gather.34.cloned.1.call-update) | async-done | bytes 8388624 | tf_op jit(solution)/shard_map/all_gather | solution.py:329
  3108.1 645.1 %all-reduce.10.cloned.1.call-done = (bf16[512,8192]{0,1:T(8,128)(2,1)}, bf16[512,16384]{1,0:T(8,128)(2,1)}, bf16[2048,2048]{1,0:T(8,128)(2,1)}) async-done(((bf16[512,8192]{0,1:T(8,128)(2,1)}, bf16[512,16384]{1,0:T(8,128)(2,1)}, bf16[2048,2048]{1,0:T(8,128)(2,1)}), (bf16[512,8192]{0,1:T(8,128)(2,1)}, bf16[512,16384]{1,0:T(8,128)(2,1)}, bf16[2048,2048]{1,0:T(8,128)(2,1)})) %all-reduce.10.cloned.1.call-update) | async-done | bytes 33554448 | tf_op jit(solution)/shard_map/psum | solution.py:348
  3753.2 16.9 fusion.100
  (392 shorter events, 370.2 us)
Async XLA Ops:
  7.2 165.3 %all-gather.16.cloned.1.call-start = ((), (), s32[]{:S(2)}) async-start(), calls=%async_computation.5 | async-start | bytes 20971520 | tf_op jit(solution)/shard_map/all_gather | solution.py:16
  12.0 160.5 %copy-start.17 = (bf16[1,256,2048]{2,1,0:T(8,128)(2,1)S(1)}, bf16[1,256,2048]{2,1,0:T(8,128)(2,1)}, u32[]{:S(2)}) copy-start(bf16[1,256,2048]{2,1,0:T(8,128)(2,1)} %param.21) | copy-start | bytes 3145732
  12.0 249.9 %all-gather.22.cloned.1.call-start = ((), (), s32[]{:S(2)}) async-start(), calls=%async_computation.8 | async-start | bytes 10485760 | tf_op jit(solution)/shard_map/all_gather | solution.py:113
  12.8 333.9 %all-gather.20.cloned.1.call-start = ((), (), s32[]{:S(2)}) async-start(), calls=%async_computation.7 | async-start | bytes 9437184 | tf_op jit(solution)/shard_map/all_gather | solution.py:153
  46.0 225.5 %copy-start.24 = (f32[256,64]{0,1:T(8,128)}, f32[256,64]{0,1:T(8,128)S(1)}, u32[]{:S(2)}) copy-start(f32[256,64]{0,1:T(8,128)S(1)} %get-tuple-element.949) | copy-start | bytes 196612
  46.0 225.5 %copy-start.26 = (f32[256,64]{0,1:T(8,128)}, f32[256,64]{0,1:T(8,128)S(1)}, u32[]{:S(2)}) copy-start(f32[256,64]{0,1:T(8,128)S(1)} %get-tuple-element.950) | copy-start | bytes 196612
  46.7 131.9 %copy-start.36 = (f32[1,2048]{1,0:T(1,128)}, f32[1,2048]{1,0:T(1,128)S(1)}, u32[]{:S(2)}) copy-start(f32[1,2048]{1,0:T(1,128)S(1)} %get-tuple-element.948) | copy-start | bytes 24580
  46.7 224.5 %copy-start.34 = (f32[1,2048]{1,0:T(1,128)}, f32[1,2048]{1,0:T(1,128)S(1)}, u32[]{:S(2)}) copy-start(f32[1,2048]{1,0:T(1,128)S(1)} %get-tuple-element.947) | copy-start | bytes 24580
  180.9 248.5 %all-gather.18.cloned.1.call-start = ((), (), s32[]{:S(2)}) async-start(), calls=%async_computation.6 | async-start | bytes 9437184 | tf_op jit(solution)/shard_map/all_gather | solution.py:154
  189.0 327.9 %all-gather.24.cloned.1.call-start = ((), (), s32[]{:S(2)}) async-start(), calls=%async_computation.9 | async-start | bytes 10485760 | tf_op jit(solution)/shard_map/all_gather | solution.py:115
  189.6 626.3 %all-gather.26.cloned.1.call-start = ((), (), s32[]{:S(2)}) async-start(), calls=%async_computation.10 | async-start | bytes 41943040 | tf_op jit(solution)/shard_map/all_gather | solution.py:206
  190.2 924.8 %all-gather.28.cloned.1.call-start = ((), (), s32[]{:S(2)}) async-start(), calls=%async_computation.11 | async-start | bytes 41943040 | tf_op jit(solution)/shard_map/all_gather | solution.py:207
  190.9 1223.1 %all-gather.30.cloned.1.call-start = ((), (), s32[]{:S(2)}) async-start(), calls=%async_computation.12 | async-start | bytes 41943040 | tf_op jit(solution)/shard_map/all_gather | solution.py:226
  191.7 1495.1 %reduce-scatter.10.cloned.1.call-start = ((), (), s32[]{:S(2)}) async-start(), calls=%async_computation.13 | async-start | bytes 9437184 | tf_op jit(solution)/shard_map/reduce_scatter | solution.py:312
  272.5 74.1 %copy-start.4 = (bf16[256,16,128]{0,2,1:T(8,128)(2,1)}, bf16[256,16,128]{0,2,1:T(8,128)(2,1)S(1)}, u32[]{:S(2)}) copy-start(bf16[256,16,128]{0,2,1:T(8,128)(2,1)S(1)} %maximum_convert_fusion) | copy-start | bytes 3145732
  472.1 51.0 %copy-start.1 = (bf16[256,2048]{1,0:T(8,128)(2,1)}, bf16[256,2048]{1,0:T(8,128)(2,1)S(1)}, u32[]{:S(2)}) copy-start(bf16[256,2048]{1,0:T(8,128)(2,1)S(1)} %get-tuple-element.1320) | copy-start | bytes 3145732
  472.1 51.0 %copy-start.30 = (bf16[2048]{0:T(1024)(128)(2,1)}, bf16[2048]{0:T(1024)(128)(2,1)S(1)}, u32[]{:S(2)}) copy-start(bf16[2048]{0:T(1024)(128)(2,1)S(1)} %get-tuple-element.1365) | copy-start | bytes 12292
  472.1 51.0 %copy-start.32 = (f32[256]{0:T(256)}, f32[256]{0:T(256)S(1)}, u32[]{:S(2)}) copy-start(f32[256]{0:T(256)S(1)} %get-tuple-element.1367) | copy-start | bytes 3076
  472.1 51.0 %copy-start.40 = (f32[16,256]{1,0:T(8,128)}, f32[16,256]{1,0:T(8,128)S(1)}, u32[]{:S(2)}) copy-start(f32[16,256]{1,0:T(8,128)S(1)} %get-tuple-element.1368) | copy-start | bytes 49156
  523.6 591.3 %copy-start.15 = (bf16[256,2048]{1,0:T(8,128)(2,1)}, bf16[256,2048]{1,0:T(8,128)(2,1)S(1)}, u32[]{:S(2)}) copy-start(bf16[256,2048]{1,0:T(8,128)(2,1)S(1)} %fusion.86) | copy-start | bytes 3145732
  1597.0 180.5 %reduce-scatter.12.cloned.1.call-start = ((), (), s32[]{:S(2)}) async-start(), calls=%async_computation.15 | async-start | bytes 9437184 | tf_op jit(solution)/shard_map/reduce_scatter | solution.py:315
  1597.6 470.0 %reduce-scatter.18.cloned.1.call-start = ((), (), s32[]{:S(2)}) async-start(), calls=%async_computation.19 | async-start | bytes 41943040
  1615.3 744.1 %reduce-scatter.14.cloned.1.call-start = ((), (), s32[]{:S(2)}) async-start(), calls=%async_computation.17 | async-start | bytes 41943040 | tf_op jit(solution)/shard_map/reduce_scatter | solution.py:338
  1624.3 63.9 %copy-start.14 = (f32[256,16,128]{0,2,1:T(8,128)S(1)}, f32[256,16,128]{0,2,1:T(8,128)}, u32[]{:S(2)}) copy-start(f32[256,16,128]{0,2,1:T(8,128)} %broadcast_multiply_fusion) | copy-start | bytes 6291460
  1624.3 63.9 %copy-start.25 = (f32[256,64]{0,1:T(8,128)S(1)}, f32[256,64]{0,1:T(8,128)}, u32[]{:S(2)}) copy-start(f32[256,64]{0,1:T(8,128)} %copy-done.24) | copy-start | bytes 196612
  1624.3 63.9 %copy-start.27 = (f32[256,64]{0,1:T(8,128)S(1)}, f32[256,64]{0,1:T(8,128)}, u32[]{:S(2)}) copy-start(f32[256,64]{0,1:T(8,128)} %copy-done.26) | copy-start | bytes 196612
  1693.4 84.1 %copy-start.19 = (bf16[1,256,2048]{2,1,0:T(8,128)(2,1)S(1)}, bf16[1,256,2048]{2,1,0:T(8,128)(2,1)}, u32[]{:S(2)}) copy-start(bf16[1,256,2048]{2,1,0:T(8,128)(2,1)} %param.21) | copy-start | bytes 3145732
  1815.2 1105.6 %reduce-scatter.16.cloned.1.call-start = ((), (), s32[]{:S(2)}) async-start(), calls=%async_computation.18 | async-start | bytes 83886080
  1845.5 1164.9 %all-gather.32.cloned.1.call-start = ((), (), s32[]{:S(2)}) async-start(), calls=%async_computation.14 | async-start | bytes 10485760 | tf_op jit(solution)/shard_map/all_gather | solution.py:328
  1846.1 1253.7 %all-gather.34.cloned.1.call-start = ((), (), s32[]{:S(2)}) async-start(), calls=%async_computation.16 | async-start | bytes 10485760 | tf_op jit(solution)/shard_map/all_gather | solution.py:329
  1846.7 1906.5 %all-reduce.10.cloned.1.call-start = ((), (), s32[]{:S(2)}) async-start(), calls=%async_computation.20 | async-start | bytes 67108864 | tf_op jit(solution)/shard_map/psum | solution.py:348
  2974.2 125.5 %copy-start.28 = (bf16[256,2048]{0,1:T(8,128)(2,1)S(1)}, bf16[256,2048]{0,1:T(8,128)(2,1)}, u32[]{:S(2)}) copy-start(bf16[256,2048]{0,1:T(8,128)(2,1)} %reduce-scatter.12.cloned.1.call-done) | copy-start | bytes 3145732
  (56 other events, 232.3 us)
Sparse Core Ops, SparseCore 0:
  12.1 160.2 all-gather.15
  174.3 87.5 all-gather.21
  264.1 82.4 all-gather.19
  348.7 80.6 all-gather.17
  431.1 85.7 all-gather.23
  518.6 297.2 all-gather.25
  817.7 297.2 all-gather.27
  1116.8 297.2 all-gather.29
  1597.1 89.5 reduce-scatter.9
  1689.5 87.9 reduce-scatter.11
  1780.6 286.9 reduce-scatter.17
  2070.8 288.6 reduce-scatter.13
  2362.5 558.2 reduce-scatter.15
  2922.5 87.8 all-gather.31
  3012.1 87.6 all-gather.33
  3102.5 650.6 all-reduce.9
